TPU v7x, 32 devices: a whole 2x2x4 slice. The times are simulated.
32 devices in a mesh: dp: 4 (over y, x), seq: 8 (over z, core).
Axes of the slice: x: 2, y: 2, z: 4, core: 2. Of those that a mesh axis runs over, the one named last changes fastest.
Arguments:
- hidden: float32 [4, 2048, 768], P('dp', 'seq'), may hold values from -6 to 6
- cotangent: float32 [4, 2048, 768], P('dp', 'seq'), may hold values from -6 to 6
- lengths: int32 [4], P('dp'), may hold values from 1024 to 2048, as said below
- norm_gain: float32 [2, 768], P(None, 'dp'), may hold values from 0.5 to 1.5
- gate_weight: float32 [2, 768, 1536], P(None, 'dp'), may hold values from -0.21875 to 0.21875
- mix_weight: float32 [2, 768, 1792], P(None, 'dp'), may hold values from -0.21875 to 0.21875
- step_weight: float32 [2, 768, 24], P(None, 'dp'), may hold values from -0.21875 to 0.21875
- conv_kernel: float32 [2, 4, 1792], P(None, None, 'dp'), may hold values from -0.5 to 0.5
- conv_bias: float32 [2, 1792], P(None, 'dp'), may hold values from -0.5 to 0.5
- gated_gain: float32 [2, 1536], P(None, 'dp'), may hold values from 0.5 to 1.5
- out_weight: float32 [2, 1536, 768], P(None, 'dp'), may hold values from -0.15625 to 0.15625
- skip_gain: float32 [2, 24], replicated, may hold values from 0.5 to 1.5
- log_rate: float32 [2, 24], replicated, may hold values from -4 to 1
- step_bias: float32 [2, 24], replicated, may hold values from -9 to -4
Outputs:
- result: float32 [4, 2048, 768], P('dp', 'seq')
- hidden_grad: float32 [4, 2048, 768], P('dp', 'seq')
- norm_gain_grad: float32 [2, 768], P(None, 'dp')
- gate_weight_grad: float32 [2, 768, 1536], P(None, 'dp')
- mix_weight_grad: float32 [2, 768, 1792], P(None, 'dp')
- step_weight_grad: float32 [2, 768, 24], P(None, 'dp')
- conv_kernel_grad: float32 [2, 4, 1792], P(None, None, 'dp')
- conv_bias_grad: float32 [2, 1792], P(None, 'dp')
- gated_gain_grad: float32 [2, 1536], P(None, 'dp')
- out_weight_grad: float32 [2, 1536, 768], P(None, 'dp')
- skip_gain_grad: float32 [2, 24], replicated
Inputs may be any that keep to these rules, and one draw needn't show every extreme that they name: `lengths`: positions at or past a slot's length are padding; some slot has length 2048 and some slot the least length.
All inputs are finite; a program needn't handle non-finite values.
Results may differ from a plain program's by a relative error of at most 0.0003.
Values sent between devices are 32-bit elements; how exact they have to be, the bound alone decides.
A program may use at most 192 MiB of HBM per device.

v0:
```python
import jax
import jax.numpy as jnp
from jax import lax
from jax.sharding import PartitionSpec as P

EPSILON = 1e-05
HIGHEST = lax.Precision.HIGHEST


def from_behind(value, axis, steps):
    count = lax.axis_size(axis)
    first, last = (max(0, -steps), min(count, count - steps))
    return lax.ppermute(value, axis, [(source, source + steps) for source in range(first, last)])


def matmul(left, right):
    return jnp.dot(left, right, precision=HIGHEST)


def rms_scale(values):
    return lax.rsqrt(jnp.mean(values * values, axis=-1, keepdims=True) + EPSILON)


def carry_forward(totals, state_local):

    def relay_turn(turn_index, incoming):
        return from_behind(totals[:, :, None, None] * incoming + state_local, "seq", 1)

    return lax.fori_loop(0, lax.axis_size("seq") - 1, relay_turn, jnp.zeros_like(state_local))


def carry_backward(totals, state_in_grad):

    def relay_back(turn_index, incoming):
        return from_behind(totals[:, :, None, None] * incoming + state_in_grad, "seq", -1)

    return lax.fori_loop(0, lax.axis_size("seq") - 1, relay_back, jnp.zeros_like(state_in_grad))


def layer_forward(stream, weights, skip_gain, log_rate, step_bias):
    (
        norm_gain,
        gate_weight,
        mix_weight,
        step_weight,
        conv_kernel,
        conv_bias,
        gated_gain,
        out_weight,
    ) = weights
    slots, group, width = stream.shape
    inner = gated_gain.shape[0]
    heads = skip_gain.shape[0]
    head_size = inner // heads
    taps = conv_kernel.shape[0]
    flat = stream.reshape(slots * group, width)
    inv_in = rms_scale(flat)
    normed = flat * inv_in * norm_gain
    gate_pre = matmul(normed, gate_weight)
    mixed_raw = matmul(normed, mix_weight).reshape(slots, group, -1)
    step_raw = matmul(normed, step_weight).reshape(slots, group, heads)
    channels = mixed_raw.shape[-1]
    states = (channels - inner) // 2
    edge = from_behind(mixed_raw[:, group - taps + 1 :, :], "seq", 1)
    extended = jnp.concatenate([edge, mixed_raw], axis=1)
    conv_pre = conv_bias
    for tap_index in range(taps):
        conv_pre = conv_pre + conv_kernel[tap_index] * extended[:, tap_index : tap_index + group, :]
    mixed = jax.nn.silu(conv_pre)
    heads_in = mixed[..., :inner].reshape(slots, group, heads, head_size)
    input_map = mixed[..., inner : inner + states]
    output_map = mixed[..., inner + states :]
    step_size = jax.nn.softplus(step_raw + step_bias)
    rates = jnp.exp(log_rate)
    log_decay = jnp.cumsum(-rates * step_size, axis=1)
    scaled_in = heads_in * step_size[..., None]
    position = lax.iota(jnp.int32, group)
    causal = (position[:, None] >= position[None, :])[None, :, :, None]
    gaps = log_decay[:, :, None, :] - log_decay[:, None, :, :]
    decays = jnp.where(causal, jnp.exp(jnp.where(causal, gaps, 0.0)), 0.0)
    intersection = jnp.einsum("btn,bsn->bts", output_map, input_map, precision=HIGHEST)
    mixing = intersection[..., None] * decays
    diag_out = jnp.einsum("btsh,bshp->bthp", mixing, scaled_in, precision=HIGHEST)
    end_weight = jnp.exp(log_decay[:, -1:, :] - log_decay)
    state_local = jnp.einsum(
        "bshp,bsn->bhpn", scaled_in * end_weight[..., None], input_map, precision=HIGHEST
    )
    totals = jnp.exp(log_decay[:, -1, :])
    state_in = carry_forward(totals, state_local)
    lift = jnp.exp(log_decay)
    off_out = lift[..., None] * jnp.einsum(
        "btn,bhpn->bthp", output_map, state_in, precision=HIGHEST
    )
    mixed_out = diag_out + off_out + skip_gain[:, None] * heads_in
    out_flat = mixed_out.reshape(slots * group, inner)
    gate_sig = jax.nn.sigmoid(gate_pre)
    gated = out_flat * (gate_pre * gate_sig)
    inv_out = rms_scale(gated)
    normed_out = gated * inv_out * gated_gain
    branch = matmul(normed_out, out_weight)
    saved = {
        "flat": flat,
        "inv_in": inv_in,
        "normed": normed,
        "gate_pre": gate_pre,
        "gate_sig": gate_sig,
        "step_raw": step_raw,
        "extended": extended,
        "conv_pre": conv_pre,
        "heads_in": heads_in,
        "input_map": input_map,
        "output_map": output_map,
        "step_size": step_size,
        "scaled_in": scaled_in,
        "decays": decays,
        "mixing": mixing,
        "end_weight": end_weight,
        "totals": totals,
        "state_in": state_in,
        "lift": lift,
        "off_out": off_out,
        "out_flat": out_flat,
        "gated": gated,
        "inv_out": inv_out,
        "normed_out": normed_out,
    }
    return (stream + branch.reshape(slots, group, width), saved)


def layer_backward(grad, saved, weights, skip_gain, log_rate, step_bias):
    (
        norm_gain,
        gate_weight,
        mix_weight,
        step_weight,
        conv_kernel,
        conv_bias,
        gated_gain,
        out_weight,
    ) = weights
    slots, group, width = grad.shape
    inner = gated_gain.shape[0]
    heads = skip_gain.shape[0]
    head_size = inner // heads
    taps = conv_kernel.shape[0]
    flat = saved["flat"]
    inv_in = saved["inv_in"]
    normed = saved["normed"]
    gate_pre = saved["gate_pre"]
    gate_sig = saved["gate_sig"]
    heads_in = saved["heads_in"]
    input_map = saved["input_map"]
    output_map = saved["output_map"]
    scaled_in = saved["scaled_in"]
    end_weight = saved["end_weight"]
    totals = saved["totals"]
    state_in = saved["state_in"]
    mixing = saved["mixing"]
    gated = saved["gated"]
    inv_out = saved["inv_out"]
    conv_pre = saved["conv_pre"]
    extended = saved["extended"]
    channels = extended.shape[-1]
    grad_flat = grad.reshape(slots * group, width)
    out_weight_grad = matmul(saved["normed_out"].T, grad_flat)
    normed_out_grad = matmul(grad_flat, out_weight.T)
    gated_gain_grad = jnp.sum(normed_out_grad * gated * inv_out, axis=0)
    scaled = normed_out_grad * gated_gain
    gated_grad = inv_out * scaled - gated * (inv_out * inv_out * inv_out) * jnp.mean(
        scaled * gated, axis=-1, keepdims=True
    )
    gate_grad = gated_grad * saved["out_flat"] * gate_sig * (1.0 + gate_pre * (1.0 - gate_sig))
    out_grad = (gated_grad * (gate_pre * gate_sig)).reshape(slots, group, heads, head_size)
    skip_grad = jnp.sum(out_grad * heads_in, axis=(0, 1, 3))
    heads_grad = skip_gain[:, None] * out_grad
    lifted_grad = out_grad * saved["lift"][..., None]
    state_in_grad = jnp.einsum("bthp,btn->bhpn", lifted_grad, output_map, precision=HIGHEST)
    output_map_grad = jnp.einsum("bthp,bhpn->btn", lifted_grad, state_in, precision=HIGHEST)
    decay_grad = jnp.sum(out_grad * saved["off_out"], axis=-1)
    pairing = jnp.einsum("bthp,bshp->btsh", out_grad, scaled_in, precision=HIGHEST)
    scaled_grad = jnp.einsum("btsh,bthp->bshp", mixing, out_grad, precision=HIGHEST)
    intersection_grad = jnp.sum(saved["decays"] * pairing, axis=-1)
    output_map_grad = output_map_grad + jnp.einsum(
        "bts,bsn->btn", intersection_grad, input_map, precision=HIGHEST
    )
    input_map_grad = jnp.einsum("bts,btn->bsn", intersection_grad, output_map, precision=HIGHEST)
    weighted = mixing * pairing
    decay_grad = decay_grad + jnp.sum(weighted, axis=2) - jnp.sum(weighted, axis=1)
    state_out_grad = carry_backward(totals, state_in_grad)
    end_grad = jnp.sum(state_out_grad * state_in, axis=(2, 3)) * totals
    reach = jnp.einsum("bhpn,bsn->bshp", state_out_grad, input_map, precision=HIGHEST)
    scaled_grad = scaled_grad + reach * end_weight[..., None]
    input_map_grad = input_map_grad + jnp.einsum(
        "bshp,bhpn->bsn", scaled_in * end_weight[..., None], state_out_grad, precision=HIGHEST
    )
    weight_pull = jnp.sum(reach * scaled_in, axis=-1) * end_weight
    end_grad = end_grad + jnp.sum(weight_pull, axis=1)
    decay_grad = decay_grad - weight_pull
    decay_grad = jnp.concatenate(
        [decay_grad[:, :-1, :], decay_grad[:, -1:, :] + end_grad[:, None, :]], axis=1
    )
    rate_grad = jnp.flip(jnp.cumsum(jnp.flip(decay_grad, axis=1), axis=1), axis=1)
    step_grad = -jnp.exp(log_rate) * rate_grad + jnp.sum(scaled_grad * heads_in, axis=-1)
    heads_grad = heads_grad + scaled_grad * saved["step_size"][..., None]
    step_raw_grad = step_grad * jax.nn.sigmoid(saved["step_raw"] + step_bias)
    mixed_grad = jnp.concatenate(
        [heads_grad.reshape(slots, group, inner), input_map_grad, output_map_grad], axis=-1
    )
    conv_sig = jax.nn.sigmoid(conv_pre)
    pre_grad = mixed_grad * conv_sig * (1.0 + conv_pre * (1.0 - conv_sig))
    conv_bias_grad = jnp.sum(pre_grad, axis=(0, 1))
    conv_kernel_grad = jnp.stack(
        [
            jnp.sum(pre_grad * extended[:, tap_index : tap_index + group, :], axis=(0, 1))
            for tap_index in range(taps)
        ]
    )
    border = jnp.zeros((slots, taps - 1, channels), jnp.float32)
    padded_grad = jnp.concatenate([border, pre_grad, border], axis=1)
    extended_grad = conv_kernel[0] * padded_grad[:, taps - 1 : taps - 1 + group + taps - 1, :]
    for tap_index in range(1, taps):
        offset = taps - 1 - tap_index
        extended_grad = (
            extended_grad
            + conv_kernel[tap_index] * padded_grad[:, offset : offset + group + taps - 1, :]
        )
    edge_back = from_behind(extended_grad[:, : taps - 1, :], "seq", -1)
    raw_grad = extended_grad[:, taps - 1 :, :]
    raw_grad = jnp.concatenate(
        [raw_grad[:, : group - taps + 1, :], raw_grad[:, group - taps + 1 :, :] + edge_back], axis=1
    )
    raw_flat = raw_grad.reshape(slots * group, channels)
    step_flat = step_raw_grad.reshape(slots * group, heads)
    gate_weight_grad = matmul(normed.T, gate_grad)
    mix_weight_grad = matmul(normed.T, raw_flat)
    step_weight_grad = matmul(normed.T, step_flat)
    normed_grad = (
        matmul(gate_grad, gate_weight.T)
        + matmul(raw_flat, mix_weight.T)
        + matmul(step_flat, step_weight.T)
    )
    norm_gain_grad = jnp.sum(normed_grad * flat * inv_in, axis=0)
    scaled_norm = normed_grad * norm_gain
    stream_grad = (
        grad_flat
        + inv_in * scaled_norm
        - flat * (inv_in * inv_in * inv_in) * jnp.mean(scaled_norm * flat, axis=-1, keepdims=True)
    )
    weight_grads = (
        norm_gain_grad,
        gate_weight_grad,
        mix_weight_grad,
        step_weight_grad,
        conv_kernel_grad,
        conv_bias_grad,
        gated_gain_grad,
        out_weight_grad,
    )
    return (stream_grad.reshape(slots, group, width), weight_grads, skip_grad)


def on_device(
    hidden,
    cotangent,
    lengths,
    norm_gain,
    gate_weight,
    mix_weight,
    step_weight,
    conv_kernel,
    conv_bias,
    gated_gain,
    out_weight,
    skip_gain,
    log_rate,
    step_bias,
):
    slots, group, width = hidden.shape
    layers = norm_gain.shape[0]
    position = lax.axis_index("seq") * group + lax.iota(jnp.int32, group)
    mask = (position[None, :] < lengths[:, None]).astype(jnp.float32)[:, :, None]
    stream = hidden
    saved_all = []
    for layer_index in range(layers):
        weights = (
            lax.all_gather(norm_gain[layer_index], "dp", axis=0, tiled=True),
            lax.all_gather(gate_weight[layer_index], "dp", axis=0, tiled=True),
            lax.all_gather(mix_weight[layer_index], "dp", axis=0, tiled=True),
            lax.all_gather(step_weight[layer_index], "dp", axis=0, tiled=True),
            lax.all_gather(conv_kernel[layer_index], "dp", axis=1, tiled=True),
            lax.all_gather(conv_bias[layer_index], "dp", axis=0, tiled=True),
            lax.all_gather(gated_gain[layer_index], "dp", axis=0, tiled=True),
            lax.all_gather(out_weight[layer_index], "dp", axis=0, tiled=True),
        )
        stream, saved = layer_forward(
            stream, weights, skip_gain[layer_index], log_rate[layer_index], step_bias[layer_index]
        )
        saved_all.append(saved)
    result = stream * mask
    grad = cotangent * mask
    reduced_all = []
    skip_all = []
    for layer_index in reversed(range(layers)):
        weights = (
            lax.all_gather(norm_gain[layer_index], "dp", axis=0, tiled=True),
            lax.all_gather(gate_weight[layer_index], "dp", axis=0, tiled=True),
            lax.all_gather(mix_weight[layer_index], "dp", axis=0, tiled=True),
            lax.all_gather(step_weight[layer_index], "dp", axis=0, tiled=True),
            lax.all_gather(conv_kernel[layer_index], "dp", axis=1, tiled=True),
            lax.all_gather(conv_bias[layer_index], "dp", axis=0, tiled=True),
            lax.all_gather(gated_gain[layer_index], "dp", axis=0, tiled=True),
            lax.all_gather(out_weight[layer_index], "dp", axis=0, tiled=True),
        )
        grad, weight_grads, skip_grad = layer_backward(
            grad,
            saved_all[layer_index],
            weights,
            skip_gain[layer_index],
            log_rate[layer_index],
            step_bias[layer_index],
        )
        reduced = (
            lax.psum_scatter(weight_grads[0], "dp", scatter_dimension=0, tiled=True),
            lax.psum_scatter(weight_grads[1], "dp", scatter_dimension=0, tiled=True),
            lax.psum_scatter(weight_grads[2], "dp", scatter_dimension=0, tiled=True),
            lax.psum_scatter(weight_grads[3], "dp", scatter_dimension=0, tiled=True),
            lax.psum_scatter(weight_grads[4], "dp", scatter_dimension=1, tiled=True),
            lax.psum_scatter(weight_grads[5], "dp", scatter_dimension=0, tiled=True),
            lax.psum_scatter(weight_grads[6], "dp", scatter_dimension=0, tiled=True),
            lax.psum_scatter(weight_grads[7], "dp", scatter_dimension=0, tiled=True),
        )
        reduced = lax.psum(
            (
                reduced[0],
                reduced[1],
                reduced[2],
                reduced[3],
                reduced[4],
                reduced[5],
                reduced[6],
                reduced[7],
            ),
            "seq",
        )
        skip_total = lax.psum(skip_grad, ("dp", "seq"))
        reduced_all.insert(0, reduced)
        skip_all.insert(0, skip_total)
    stacked = tuple((jnp.stack([entry[member] for entry in reduced_all]) for member in range(8)))
    return (result, grad) + stacked + (jnp.stack(skip_all),)


def solution(mesh):
    return jax.shard_map(
        on_device,
        mesh=mesh,
        in_specs=(
            P("dp", "seq", None),
            P("dp", "seq", None),
            P("dp"),
            P(None, "dp"),
            P(None, "dp", None),
            P(None, "dp", None),
            P(None, "dp", None),
            P(None, None, "dp"),
            P(None, "dp"),
            P(None, "dp"),
            P(None, "dp", None),
            P(),
            P(),
            P(),
        ),
        out_specs=(
            P("dp", "seq", None),
            P("dp", "seq", None),
            P(None, "dp"),
            P(None, "dp", None),
            P(None, "dp", None),
            P(None, "dp", None),
            P(None, None, "dp"),
            P(None, "dp"),
            P(None, "dp"),
            P(None, "dp", None),
            P(),
        ),
        check_vma=False,
    )
```

profile of v0, /device:TPU:0, one launch (start us, length us, event | category | flops | bytes accessed | tf_op | source)
XLA Modules:
  0.0 1350.7 jit_solution(13960874902507613550)
XLA Ops:
  17.8 14.1 %all-gather.4 = f32[1,768,24]{2,0,1:T(1,128)S(1)} all-gather(f32[1,192,24]{2,0,1:T(1,128)S(1)} %copy.514), channel_id=6, replica_groups=mesh['dp'=4,'seq'=8] {'dp'}, dimensions={1}, use_global_device_ids=true | all-gather | bytes 92160 | tf_op jit(solution)/shard_map/all_gather | solution.py:289
  36.6 16.4 %all-reduce.18 = (f32[768]{0:T(1024)S(1)}, f32[1792]{0:T(1024)}, f32[768]{0:T(1024)S(1)}, f32[1792]{0:T(1024)}) all-reduce(f32[768]{0:T(1024)S(1)} %dynamic-update-slice.1, f32[1792]{0:T(1024)S(1)} %dynamic-update-slice, f32[768]{0:T(1024)S(1)} %dynamic-update-slice.3, ...), channel_id=4, replica_groups=mesh['dp'=4,'seq'=8] {'dp'}, use_global_device_ids=true, to_apply=%add.5 | all-reduce | flops 5120 | bytes 40960 | tf_op jit(solution)/shard_map/all_gather | solution.py:286
  56.2 20.5 %all-gather.1 = f32[1,4,1792]{1,0,2:T(1,128)S(1)} all-gather(f32[1,4,448]{1,0,2:T(1,128)S(1)} %copy.513), channel_id=3, replica_groups=mesh['dp'=4,'seq'=8] {'dp'}, dimensions={2}, use_global_device_ids=true | all-gather | bytes 35840 | tf_op jit(solution)/shard_map/all_gather | solution.py:290
  76.8 37.7 %slice_reduce_fusion.7 = (f32[1792]{0:T(1024)}, f32[1792]{0:T(1024)}, f32[1792]{0:T(1024)}, f32[1792]{0:T(1024)}) fusion(f32[1,4,1792]{1,0,2:T(1,128)S(1)} %all-gather.1), kind=kLoop, calls=%fused_computation.195 | loop fusion | bytes 57344 | tf_op jit(solution)/shard_map/slice | solution.py:68
  115.3 17.0 %all-gather.9 = f32[1,4,1792]{1,0,2:T(1,128)S(1)} all-gather(f32[1,4,448]{1,0,2:T(1,128)S(1)} %copy.515), channel_id=11, replica_groups=mesh['dp'=4,'seq'=8] {'dp'}, dimensions={2}, use_global_device_ids=true | all-gather | bytes 35840 | tf_op jit(solution)/shard_map/all_gather | solution.py:290
  132.3 37.9 %slice_reduce_fusion.3 = (f32[1792]{0:T(1024)}, f32[1792]{0:T(1024)}, f32[1792]{0:T(1024)}, f32[1792]{0:T(1024)}) fusion(f32[1,4,1792]{1,0,2:T(1,128)S(1)} %all-gather.9), kind=kLoop, calls=%fused_computation.191 | loop fusion | bytes 57344 | tf_op jit(solution)/shard_map/slice | solution.py:68
  229.8 90.3 %while.40 = (s32[]{:T(128)}, f32[1,24,64,128]{3,2,1,0:T(8,128)S(1)}, f32[1,24]{1,0:T(1,128)}, f32[1,24,64,128]{3,2,1,0:T(8,128)S(1)}, s32[]{:T(128)}) while((s32[]{:T(128)}, f32[1,24,64,128]{3,2,1,0:T(8,128)S(1)}, f32[1,24]{1,0:T(1,128)}, f32[1,24,64,128]{3,2,1,0:T(8,128)S(1)}, s32[]{:T(128)}) %tuple.134), condition=%wide.region_4.5_spmd, body=%wide.region_3.4_spmd.sunk | while | flops 393218 | bytes 5505221 | solution.py:29
  405.7 100.9 %while.41 = (s32[]{:T(128)}, f32[1,24,64,128]{3,2,1,0:T(8,128)S(1)}, f32[1,24]{1,0:T(1,128)}, f32[1,24,64,128]{3,2,1,0:T(8,128)}, s32[]{:T(128)}) while((s32[]{:T(128)}, f32[1,24,64,128]{3,2,1,0:T(8,128)S(1)}, f32[1,24]{1,0:T(1,128)}, f32[1,24,64,128]{3,2,1,0:T(8,128)}, s32[]{:T(128)}) %tuple.137), condition=%wide.region_10.11_spmd, body=%wide.region_9.10_spmd.sunk | while | flops 393218 | bytes 5505221 | solution.py:29
  571.8 114.4 %while.42 = (s32[]{:T(128)}, f32[1,24,64,128]{3,2,1,0:T(8,128)}, f32[1,24]{1,0:T(1,128)}, f32[1,24,64,128]{3,2,1,0:T(8,128)}, s32[]{:T(128)}) while((s32[]{:T(128)}, f32[1,24,64,128]{3,2,1,0:T(8,128)}, f32[1,24]{1,0:T(1,128)}, f32[1,24,64,128]{3,2,1,0:T(8,128)}, s32[]{:T(128)}) %tuple.182), condition=%wide.region_14.15_spmd, body=%wide.region_13.14_spmd.sunk | while | flops 393218 | bytes 5505221 | solution.py:37
  591.7 13.3 collective-permute-done.2
  608.6 12.6 collective-permute-done.2
  624.9 12.6 collective-permute-done.2
  641.2 12.7 collective-permute-done.2
  657.7 12.5 collective-permute-done.2
  823.5 111.6 %while.43 = (s32[]{:T(128)}, f32[1,24,64,128]{3,2,1,0:T(8,128)S(1)}, f32[1,24]{1,0:T(1,128)S(1)}, f32[1,24,64,128]{3,2,1,0:T(8,128)}, s32[]{:T(128)}) while((s32[]{:T(128)}, f32[1,24,64,128]{3,2,1,0:T(8,128)S(1)}, f32[1,24]{1,0:T(1,128)S(1)}, f32[1,24,64,128]{3,2,1,0:T(8,128)}, s32[]{:T(128)}) %tuple.181), condition=%wide.region_28.29_spmd, body=%wide.region_27.28_spmd.sunk | while | flops 393218 | bytes 5505221 | solution.py:37
  843.1 12.7 collective-permute-done.3
  874.9 12.6 collective-permute-done.3
  922.5 12.6 collective-permute-done.3
  1005.1 51.9 %reduce-scatter.23.cloned.1.call-done = f32[192,1792]{1,0:T(8,128)} async-done(((f32[768,1792]{1,0:T(8,128)}), f32[192,1792]{1,0:T(8,128)}) %reduce-scatter.23.cloned.1.call-update) | async-done | bytes 1376272 | tf_op jit(solution)/shard_map/reduce_scatter | solution.py:325
  1066.8 39.6 %all-reduce.14 = (f32[1,24]{1,0:T(1,128)S(1)}, f32[1,24]{1,0:T(1,128)S(1)}) all-reduce(f32[1,24]{1,0:T(1,128)S(1)} %bitcast.663, f32[1,24]{1,0:T(1,128)S(1)} %bitcast.664), channel_id=1, replica_groups=mesh['dp'=4,'seq'=8] {'dp','seq'}, use_global_device_ids=true, to_apply=%region_91.92 | all-reduce | flops 48 | bytes 384 | tf_op jit(solution)/shard_map/psum | solution.py:345
  1122.7 17.5 %all-reduce.17 = (f32[768]{0:T(1024)S(1)}, f32[768]{0:T(1024)S(1)}, f32[1792]{0:T(1024)S(1)}, f32[1792]{0:T(1024)S(1)}, f32[1536]{0:T(1024)S(1)}, /*index=5*/f32[1536]{0:T(1024)S(1)}) all-reduce(f32[768]{0:T(1024)S(1)} %copy-done.142, f32[768]{0:T(1024)S(1)} %get-tuple-element.129, ...), channel_id=19, replica_groups=mesh['dp'=4,'seq'=8] {'dp'}, use_global_device_ids=true, to_apply=%region_44.45.clone | all-reduce | flops 8192 | bytes 65536
  1146.3 26.1 %reduce-scatter.31.cloned.1.call-done = f32[192,24]{1,0:T(8,128)} async-done(((f32[768,24]{1,0:T(8,128)}), f32[192,24]{1,0:T(8,128)}) %reduce-scatter.31.cloned.1.call-update) | async-done | bytes 18448
  1173.3 31.6 %all-reduce.15 = (f32[1,192]{1,0:T(1,128)S(1)}, f32[1,192]{1,0:T(1,128)S(1)}, f32[1,192,24]{1,2,0:T(8,128)S(1)}, f32[1,192,24]{1,2,0:T(8,128)S(1)}, f32[1,4,448]...) all-reduce(f32[1,192]{1,0:T(1,128)S(1)} %bitcast.655, ...), channel_id=1, replica_groups=mesh['dp'=4,'seq'=8] {'seq'}, use_global_device_ids=true, to_apply=%region_45.46 | all-reduce | flops 14848 | bytes 118784 | tf_op jit(solution)/shard_map/psum | solution.py:332
  1207.9 128.5 %all-reduce.21.cloned.1.call-done = (f32[1,192,1536]{2,1,0:T(8,128)}, f32[1,192,1536]{2,1,0:T(8,128)}, f32[1,192,1792]{2,1,0:T(8,128)}, f32[1,192,1792]{2,1,0:T(...) async-done(((f32[1,192,1536]{2,1,0:T(8,128)}, f32[1,192,1536]{2,1,0:T(8,128)}, f32[1,192,1792]{2,1,0:T(8,128)}, f32[1,192,1792]{2,1,0:T(8,128)}, ...) | async-done | bytes 7471120 | tf_op jit(solution)/shard_map/psum | solution.py:332
  (728 shorter events, 788.2 us)
Async XLA Ops:
  7.2 163.7 %all-gather.23.cloned.1.call-start = ((), (), s32[]{:S(2)}) async-start(), calls=%async_computation.16 | async-start | bytes 6881280 | tf_op jit(solution)/shard_map/all_gather | solution.py:288
  10.9 323.2 %all-gather.25.cloned.1.call-start = ((), (), s32[]{:S(2)}) async-start(), calls=%async_computation.17 | async-start | bytes 5898240 | tf_op jit(solution)/shard_map/all_gather | solution.py:287
  12.5 331.4 %all-gather.27.cloned.1.call-start = ((), (), s32[]{:S(2)}) async-start(), calls=%async_computation.18 | async-start | bytes 5898240 | tf_op jit(solution)/shard_map/all_gather | solution.py:293
  15.8 338.2 %all-gather.29.cloned.1.call-start = ((), (), s32[]{:S(2)}) async-start(), calls=%async_computation.19 | async-start | bytes 6881280 | tf_op jit(solution)/shard_map/all_gather | solution.py:288
  16.4 504.2 %all-gather.31.cloned.1.call-start = ((), (), s32[]{:S(2)}) async-start(), calls=%async_computation.20 | async-start | bytes 5898240 | tf_op jit(solution)/shard_map/all_gather | solution.py:287
  17.0 513.9 %all-gather.33.cloned.1.call-start = ((), (), s32[]{:S(2)}) async-start(), calls=%async_computation.21 | async-start | bytes 5898240 | tf_op jit(solution)/shard_map/all_gather | solution.py:293
  17.6 987.4 %reduce-scatter.21.cloned.1.call-start = ((), (), s32[]{:S(2)}) async-start(), calls=%async_computation.11 | async-start | bytes 5898240 | tf_op jit(solution)/shard_map/reduce_scatter | solution.py:324
  179.0 37.5 %collective-permute-start.4 = (f32[1,3,1792]{2,1,0:T(4,128)}, f32[1,3,1792]{2,1,0:T(4,128)S(1)}, u32[]{:S(2)}, u32[]{:S(2)}) collective-permute-start(f32[1,3,1792]{2,1,0:T(4,128)} %slice.331), channel_id=1, source_target_pairs={{0,1},{1,2},{2,3},{3,4},{4,5},{5,6},{6,7},{8,9},{9,10},{10,11},{11... | collective-permute-start | bytes 64520 | tf_op jit(solution)/shard_map/ppermute | solution.py:13
  235.1 14.3 %collective-permute-start = (f32[1,24,64,128]{3,2,1,0:T(8,128)S(1)}, f32[1,24,64,128]{3,2,1,0:T(8,128)S(1)}, u32[]{:S(2)}, u32[]{:S(2)}) collective-permute-start(f32[1,24,64,128]{3,2,1,0:T(8,128)S(1)} %multiply_add_fusion.10), channel_id=1, source_target_pairs={{0,1},{1,2},{2,3},{3,4},{4,5},{5,6},{6,7},{8,9},{9,10},{10,11},{11... | collective-permute-start | bytes 2359304 | tf_op jit(solution)/shard_map/while/body/eval_jaxpr/ppermute | solution.py:13
  362.6 23.0 %collective-permute-start.5 = (f32[1,3,1792]{2,1,0:T(4,128)S(1)}, f32[1,3,1792]{2,1,0:T(4,128)S(1)}, u32[]{:S(2)}, u32[]{:S(2)}) collective-permute-start(f32[1,3,1792]{2,1,0:T(4,128)S(1)} %slice.345), channel_id=1, source_target_pairs={{0,1},{1,2},{2,3},{3,4},{4,5},{5,6},{6,7},{8,9},{9,10},{10,11},{11... | collective-permute-start | bytes 64520 | tf_op jit(solution)/shard_map/ppermute | solution.py:13
  549.3 455.7 %reduce-scatter.29.cloned.1.call-start = ((), (), s32[]{:S(2)}) async-start(), calls=%async_computation.15 | async-start | bytes 5898240 | tf_op jit(solution)/shard_map/reduce_scatter | solution.py:330
  570.8 434.3 %reduce-scatter.19.cloned.1.call-start = ((), (), s32[]{:S(2)}) async-start(), calls=%async_computation.10 | async-start | bytes 5898240 | tf_op jit(solution)/shard_map/reduce_scatter | solution.py:324
  590.4 14.6 %collective-permute-start.2 = (f32[1,24,64,128]{3,2,1,0:T(8,128)}, f32[1,24,64,128]{3,2,1,0:T(8,128)}, u32[]{:S(2)}, u32[]{:S(2)}) collective-permute-start(f32[1,24,64,128]{3,2,1,0:T(8,128)} %multiply_add_fusion.12), channel_id=1, source_target_pairs={{1,0},{2,1},{3,2},{4,3},{5,4},{6,5},{7,6},{9,8},{10,9},{11,10},{12... | collective-permute-start | bytes 2359304 | tf_op jit(solution)/shard_map/while/body/eval_jaxpr/ppermute | solution.py:13
  639.9 14.0 %collective-permute-start.2 = (f32[1,24,64,128]{3,2,1,0:T(8,128)}, f32[1,24,64,128]{3,2,1,0:T(8,128)}, u32[]{:S(2)}, u32[]{:S(2)}) collective-permute-start(f32[1,24,64,128]{3,2,1,0:T(8,128)} %multiply_add_fusion.12), channel_id=1, source_target_pairs={{1,0},{2,1},{3,2},{4,3},{5,4},{6,5},{7,6},{9,8},{10,9},{11,10},{12... | collective-permute-start | bytes 2359304 | tf_op jit(solution)/shard_map/while/body/eval_jaxpr/ppermute | solution.py:13
  737.2 23.4 %collective-permute-start.6 = (f32[1,3,1792]{2,1,0:T(4,128)}, f32[1,3,1792]{2,1,0:T(4,128)}, u32[]{:S(2)}, u32[]{:S(2)}) collective-permute-start(f32[1,3,1792]{2,1,0:T(4,128)} %slice.362), channel_id=1, source_target_pairs={{1,0},{2,1},{3,2},{4,3},{5,4},{6,5},{7,6},{9,8},{10,9},{11,10},{12... | collective-permute-start | bytes 64520 | tf_op jit(solution)/shard_map/ppermute | solution.py:13
  787.3 217.7 %reduce-scatter.27.cloned.1.call-start = ((), (), s32[]{:S(2)}) async-start(), calls=%async_computation.14 | async-start | bytes 5898240 | tf_op jit(solution)/shard_map/reduce_scatter | solution.py:330
  795.0 210.1 %reduce-scatter.25.cloned.1.call-start = ((), (), s32[]{:S(2)}) async-start(), calls=%async_computation.13 | async-start | bytes 6881280 | tf_op jit(solution)/shard_map/reduce_scatter | solution.py:325
  803.7 253.3 %reduce-scatter.23.cloned.1.call-start = ((), (), s32[]{:S(2)}) async-start(), calls=%async_computation.12 | async-start | bytes 6881280 | tf_op jit(solution)/shard_map/reduce_scatter | solution.py:325
  841.8 14.0 %collective-permute-start.3 = (f32[1,24,64,128]{3,2,1,0:T(8,128)}, f32[1,24,64,128]{3,2,1,0:T(8,128)S(1)}, u32[]{:S(2)}, u32[]{:S(2)}) collective-permute-start(f32[1,24,64,128]{3,2,1,0:T(8,128)} %multiply_add_fusion.13), channel_id=1, source_target_pairs={{1,0},{2,1},{3,2},{4,3},{5,4},{6,5},{7,6},{9,8},{10,9},{11,10},{12... | collective-permute-start | bytes 2359304 | tf_op jit(solution)/shard_map/while/body/eval_jaxpr/ppermute | solution.py:13
  991.9 149.9 %reduce-scatter.37.cloned.1.call-start = ((), (), s32[]{:S(2)}) async-start(), calls=%async_computation.25 | async-start | bytes 1146880
  994.0 148.9 %reduce-scatter.35.cloned.1.call-start = ((), (), s32[]{:S(2)}) async-start(), calls=%async_computation.24 | async-start | bytes 1146880
  995.4 149.9 %reduce-scatter.33.cloned.1.call-start = ((), (), s32[]{:S(2)}) async-start(), calls=%async_computation.23 | async-start | bytes 491520
  997.7 174.7 %reduce-scatter.31.cloned.1.call-start = ((), (), s32[]{:S(2)}) async-start(), calls=%async_computation.22 | async-start | bytes 491520
  1004.9 331.5 %all-reduce.21.cloned.1.call-start = ((), (), s32[]{:S(2)}) async-start(), calls=%async_computation.26 | async-start | bytes 14942208 | tf_op jit(solution)/shard_map/psum | solution.py:332
  (195 other events, 2256.9 us)
Sparse Core Ops, SparseCore 0:
  11.0 76.4 all-gather.22
  89.3 60.2 all-gather.24
  151.5 57.4 all-gather.26
  210.7 65.1 all-gather.28
  277.6 57.0 all-gather.30
  336.4 57.0 all-gather.32
  549.4 66.9 reduce-scatter.20
  619.4 57.0 reduce-scatter.28
  787.5 66.5 reduce-scatter.18
  856.9 57.0 reduce-scatter.26
  917.1 63.6 reduce-scatter.24
  992.0 64.8 reduce-scatter.22
  1060.5 27.1 reduce-scatter.36
  1091.0 27.0 reduce-scatter.34
  1120.7 24.5 reduce-scatter.32
  1148.0 24.3 reduce-scatter.30
  1175.1 161.2 all-reduce.20
where the time goes:
time: 1360 us; the launch traced here: 1350 us
  waiting for transfers between devices  424 us (31%)
  matrix products  246 us (18%)
  local copies, waits for them, and re-layouts  189 us (14%)
  blocking collectives  181 us (13%)
  starting transfers between devices  176 us (13%)
  other arithmetic  112 us (8%)
  between operations  20.5 us (2%)
    ppermute x32, waiting for transfers between devices, from_behind(): lax.ppermute(value, axis, [(source, source + steps) for source in range(f...  214 us
    ppermute x32, starting transfers between devices, from_behind(): lax.ppermute(value, axis, [(source, source + steps) for source in range(f...  175 us
    dot_general x22, matrix products, matmul(): return jnp.dot(left, right, precision=HIGHEST)  136 us
    psum x1, waiting for transfers between devices, on_device(): lax.psum((reduced[0], reduced[1], reduced[2], reduced[3], reduced[4], red...  128 us
    slice x2, local copies, waits for them, and re-layouts, layer_forward(): conv_kernel[tap_index] * extended[:, tap_index:tap_index + group, :]  75.7 us
    reduce_scatter x2, waiting for transfers between devices, on_device(): lax.psum_scatter(weight_grads[2], 'dp', scatter_dimension=0, tiled=True)  51.9 us
    psum x1, blocking collectives, on_device(): skip_total = lax.psum(skip_grad, ('dp', 'seq'))  39.6 us
    all_gather x2, blocking collectives, on_device(): lax.all_gather(conv_kernel[layer_index], 'dp', axis=1, tiled=True)  37.6 us
  transfers between devices with their start and end apart: 49, of which 33 were waited for; matrix products, arithmetic and copies ran while one was open for 38% of the time, Pallas kernels for 0%

commit v1 on v0

--- a/solution.py
+++ b/solution.py
@@ -342,7 +342,7 @@
             ),
             "seq",
         )
-        skip_total = lax.psum(skip_grad, ("dp", "seq"))
+        skip_total = jnp.sum(lax.all_gather(skip_grad, ("dp", "seq")), axis=0)
         reduced_all.insert(0, reduced)
         skip_all.insert(0, skip_total)
     stacked = tuple((jnp.stack([entry[member] for entry in reduced_all]) for member in range(8)))

time: 1360 us -> 1360 us (level)
    psum x1 -> x0, blocking collectives: 39.6 us -> none  [on_device(): skip_total = lax.psum(skip_grad, ('dp', 'seq'))]
    unnamed x1 -> x2, blocking collectives: 17.5 us -> 56.9 us
where the time goes in v1:
time: 1360 us; the launch traced here: 1350 us
  waiting for transfers between devices  423 us (31%)
  matrix products  248 us (18%)
  local copies, waits for them, and re-layouts  190 us (14%)
  blocking collectives  180 us (13%)
  starting transfers between devices  176 us (13%)
  other arithmetic  115 us (8%)
  between operations  20.6 us (2%)
    ppermute x32, waiting for transfers between devices, from_behind(): lax.ppermute(value, axis, [(source, source + steps) for source in range(f...  214 us
    ppermute x32, starting transfers between devices, from_behind(): lax.ppermute(value, axis, [(source, source + steps) for source in range(f...  175 us
    dot_general x22, matrix products, matmul(): return jnp.dot(left, right, precision=HIGHEST)  137 us
    psum x1, waiting for transfers between devices, on_device(): lax.psum((reduced[0], reduced[1], reduced[2], reduced[3], reduced[4], red...  128 us
    slice x2, local copies, waits for them, and re-layouts, layer_forward(): conv_kernel[tap_index] * extended[:, tap_index:tap_index + group, :]  75.7 us
    unnamed x2, blocking collectives  56.9 us
    reduce_scatter x2, waiting for transfers between devices, on_device(): lax.psum_scatter(weight_grads[2], 'dp', scatter_dimension=0, tiled=True)  51.9 us
    all_gather x2, blocking collectives, on_device(): lax.all_gather(conv_kernel[layer_index], 'dp', axis=1, tiled=True)  36.3 us
  transfers between devices with their start and end apart: 49, of which 33 were waited for; matrix products, arithmetic and copies ran while one was open for 38% of the time, Pallas kernels for 0%

profile of v1, /device:TPU:0, one launch (start us, length us, event | category | flops | bytes accessed | tf_op | source)
XLA Modules:
  0.0 1353.5 jit_solution(4864058043749203314)
XLA Ops:
  17.8 14.1 %all-gather.4 = f32[1,768,24]{2,0,1:T(1,128)S(1)} all-gather(f32[1,192,24]{2,0,1:T(1,128)S(1)} %copy.514), channel_id=6, replica_groups=mesh['dp'=4,'seq'=8] {'dp'}, dimensions={1}, use_global_device_ids=true | all-gather | bytes 92160 | tf_op jit(solution)/shard_map/all_gather | solution.py:289
  36.6 16.3 %all-reduce.20 = (f32[768]{0:T(1024)S(1)}, f32[1792]{0:T(1024)}, f32[768]{0:T(1024)S(1)}, f32[1792]{0:T(1024)}) all-reduce(f32[768]{0:T(1024)S(1)} %dynamic-update-slice.1, f32[1792]{0:T(1024)S(1)} %dynamic-update-slice, f32[768]{0:T(1024)S(1)} %dynamic-update-slice.3, ...), channel_id=4, replica_groups=mesh['dp'=4,'seq'=8] {'dp'}, use_global_device_ids=true, to_apply=%add.5 | all-reduce | flops 5120 | bytes 40960 | tf_op jit(solution)/shard_map/all_gather | solution.py:286
  56.2 20.5 %all-gather.1 = f32[1,4,1792]{1,0,2:T(1,128)S(1)} all-gather(f32[1,4,448]{1,0,2:T(1,128)S(1)} %copy.513), channel_id=3, replica_groups=mesh['dp'=4,'seq'=8] {'dp'}, dimensions={2}, use_global_device_ids=true | all-gather | bytes 35840 | tf_op jit(solution)/shard_map/all_gather | solution.py:290
  76.7 37.7 %slice_reduce_fusion.7 = (f32[1792]{0:T(1024)}, f32[1792]{0:T(1024)}, f32[1792]{0:T(1024)}, f32[1792]{0:T(1024)}) fusion(f32[1,4,1792]{1,0,2:T(1,128)S(1)} %all-gather.1), kind=kLoop, calls=%fused_computation.195 | loop fusion | bytes 57344 | tf_op jit(solution)/shard_map/slice | solution.py:68
  115.2 15.8 %all-gather.9 = f32[1,4,1792]{1,0,2:T(1,128)S(1)} all-gather(f32[1,4,448]{1,0,2:T(1,128)S(1)} %copy.515), channel_id=11, replica_groups=mesh['dp'=4,'seq'=8] {'dp'}, dimensions={2}, use_global_device_ids=true | all-gather | bytes 35840 | tf_op jit(solution)/shard_map/all_gather | solution.py:290
  131.0 37.9 %slice_reduce_fusion.3 = (f32[1792]{0:T(1024)}, f32[1792]{0:T(1024)}, f32[1792]{0:T(1024)}, f32[1792]{0:T(1024)}) fusion(f32[1,4,1792]{1,0,2:T(1,128)S(1)} %all-gather.9), kind=kLoop, calls=%fused_computation.191 | loop fusion | bytes 57344 | tf_op jit(solution)/shard_map/slice | solution.py:68
  229.7 89.9 %while.40 = (s32[]{:T(128)}, f32[1,24,64,128]{3,2,1,0:T(8,128)S(1)}, f32[1,24]{1,0:T(1,128)}, f32[1,24,64,128]{3,2,1,0:T(8,128)S(1)}, s32[]{:T(128)}) while((s32[]{:T(128)}, f32[1,24,64,128]{3,2,1,0:T(8,128)S(1)}, f32[1,24]{1,0:T(1,128)}, f32[1,24,64,128]{3,2,1,0:T(8,128)S(1)}, s32[]{:T(128)}) %tuple.134), condition=%wide.region_4.5_spmd, body=%wide.region_3.4_spmd.sunk | while | flops 393218 | bytes 5505221 | solution.py:29
  406.0 100.7 %while.41 = (s32[]{:T(128)}, f32[1,24,64,128]{3,2,1,0:T(8,128)S(1)}, f32[1,24]{1,0:T(1,128)}, f32[1,24,64,128]{3,2,1,0:T(8,128)}, s32[]{:T(128)}) while((s32[]{:T(128)}, f32[1,24,64,128]{3,2,1,0:T(8,128)S(1)}, f32[1,24]{1,0:T(1,128)}, f32[1,24,64,128]{3,2,1,0:T(8,128)}, s32[]{:T(128)}) %tuple.137), condition=%wide.region_10.11_spmd, body=%wide.region_9.10_spmd.sunk | while | flops 393218 | bytes 5505221 | solution.py:29
  571.9 114.2 %while.42 = (s32[]{:T(128)}, f32[1,24,64,128]{3,2,1,0:T(8,128)}, f32[1,24]{1,0:T(1,128)}, f32[1,24,64,128]{3,2,1,0:T(8,128)}, s32[]{:T(128)}) while((s32[]{:T(128)}, f32[1,24,64,128]{3,2,1,0:T(8,128)}, f32[1,24]{1,0:T(1,128)}, f32[1,24,64,128]{3,2,1,0:T(8,128)}, s32[]{:T(128)}) %tuple.182), condition=%wide.region_14.15_spmd, body=%wide.region_13.14_spmd.sunk | while | flops 393218 | bytes 5505221 | solution.py:37
  591.8 13.0 collective-permute-done.2
  608.5 12.6 collective-permute-done.2
  624.8 12.6 collective-permute-done.2
  641.1 12.7 collective-permute-done.2
  825.9 111.9 %while.43 = (s32[]{:T(128)}, f32[1,24,64,128]{3,2,1,0:T(8,128)S(1)}, f32[1,24]{1,0:T(1,128)S(1)}, f32[1,24,64,128]{3,2,1,0:T(8,128)}, s32[]{:T(128)}) while((s32[]{:T(128)}, f32[1,24,64,128]{3,2,1,0:T(8,128)S(1)}, f32[1,24]{1,0:T(1,128)S(1)}, f32[1,24,64,128]{3,2,1,0:T(8,128)}, s32[]{:T(128)}) %tuple.181), condition=%wide.region_28.29_spmd, body=%wide.region_27.28_spmd.sunk | while | flops 393218 | bytes 5505221 | solution.py:37
  829.8 12.6 collective-permute-done.3
  845.8 12.6 collective-permute-done.3
  877.6 12.6 collective-permute-done.3
  925.2 12.6 collective-permute-done.3
  1008.0 51.9 %reduce-scatter.23.cloned.1.call-done = f32[192,1792]{1,0:T(8,128)} async-done(((f32[768,1792]{1,0:T(8,128)}), f32[192,1792]{1,0:T(8,128)}) %reduce-scatter.23.cloned.1.call-update) | async-done | bytes 1376272 | tf_op jit(solution)/shard_map/reduce_scatter | solution.py:325
  1070.4 39.6 %all-reduce.16 = (f32[768]{0:T(1024)S(1)}, f32[768]{0:T(1024)S(1)}) all-reduce(f32[768]{0:T(1024)S(1)} %dynamic-update-slice.5, f32[768]{0:T(1024)S(1)} %dynamic-update-slice.4), channel_id=19, replica_groups=mesh['dp'=4,'seq'=8] {'dp','seq'}, use_global_device_ids=true, to_apply=%add.9 | all-reduce | flops 1536 | bytes 12288
  1126.5 17.3 %all-reduce.19 = (f32[768]{0:T(1024)S(1)}, f32[768]{0:T(1024)S(1)}, f32[1792]{0:T(1024)S(1)}, f32[1792]{0:T(1024)S(1)}, f32[1536]{0:T(1024)S(1)}, /*index=5*/f32[1536]{0:T(1024)S(1)}) all-reduce(f32[768]{0:T(1024)S(1)} %copy-done.140, f32[768]{0:T(1024)S(1)} %get-tuple-element.129, ...), channel_id=21, replica_groups=mesh['dp'=4,'seq'=8] {'dp'}, use_global_device_ids=true, to_apply=%region_44.45.clone | all-reduce | flops 8192 | bytes 65536
  1149.0 26.1 %reduce-scatter.31.cloned.1.call-done = f32[192,24]{1,0:T(8,128)} async-done(((f32[768,24]{1,0:T(8,128)}), f32[192,24]{1,0:T(8,128)}) %reduce-scatter.31.cloned.1.call-update) | async-done | bytes 18448
  1176.1 31.6 %all-reduce.17 = (f32[1,192]{1,0:T(1,128)S(1)}, f32[1,192]{1,0:T(1,128)S(1)}, f32[1,192,24]{1,2,0:T(8,128)S(1)}, f32[1,192,24]{1,2,0:T(8,128)S(1)}, f32[1,4,448]...) all-reduce(f32[1,192]{1,0:T(1,128)S(1)} %bitcast.652, ...), channel_id=1, replica_groups=mesh['dp'=4,'seq'=8] {'seq'}, use_global_device_ids=true, to_apply=%region_45.46 | all-reduce | flops 14848 | bytes 118784 | tf_op jit(solution)/shard_map/psum | solution.py:332
  1210.7 128.5 %all-reduce.23.cloned.1.call-done = (f32[1,192,1536]{2,1,0:T(8,128)}, f32[1,192,1536]{2,1,0:T(8,128)}, f32[1,192,1792]{2,1,0:T(8,128)}, f32[1,192,1792]{2,1,0:T(...) async-done(((f32[1,192,1536]{2,1,0:T(8,128)}, f32[1,192,1536]{2,1,0:T(8,128)}, f32[1,192,1792]{2,1,0:T(8,128)}, f32[1,192,1792]{2,1,0:T(8,128)}, ...) | async-done | bytes 7471120 | tf_op jit(solution)/shard_map/psum | solution.py:332
  (732 shorter events, 792.6 us)
Async XLA Ops:
  7.2 162.4 %all-gather.25.cloned.1.call-start = ((), (), s32[]{:S(2)}) async-start(), calls=%async_computation.16 | async-start | bytes 6881280 | tf_op jit(solution)/shard_map/all_gather | solution.py:288
  10.9 322.8 %all-gather.27.cloned.1.call-start = ((), (), s32[]{:S(2)}) async-start(), calls=%async_computation.17 | async-start | bytes 5898240 | tf_op jit(solution)/shard_map/all_gather | solution.py:287
  12.5 331.0 %all-gather.29.cloned.1.call-start = ((), (), s32[]{:S(2)}) async-start(), calls=%async_computation.18 | async-start | bytes 5898240 | tf_op jit(solution)/shard_map/all_gather | solution.py:293
  15.8 338.0 %all-gather.31.cloned.1.call-start = ((), (), s32[]{:S(2)}) async-start(), calls=%async_computation.19 | async-start | bytes 6881280 | tf_op jit(solution)/shard_map/all_gather | solution.py:288
  16.4 504.4 %all-gather.33.cloned.1.call-start = ((), (), s32[]{:S(2)}) async-start(), calls=%async_computation.20 | async-start | bytes 5898240 | tf_op jit(solution)/shard_map/all_gather | solution.py:287
  17.0 514.1 %all-gather.35.cloned.1.call-start = ((), (), s32[]{:S(2)}) async-start(), calls=%async_computation.21 | async-start | bytes 5898240 | tf_op jit(solution)/shard_map/all_gather | solution.py:293
  17.6 990.3 %reduce-scatter.21.cloned.1.call-start = ((), (), s32[]{:S(2)}) async-start(), calls=%async_computation.11 | async-start | bytes 5898240 | tf_op jit(solution)/shard_map/reduce_scatter | solution.py:324
  177.6 38.7 %collective-permute-start.4 = (f32[1,3,1792]{2,1,0:T(4,128)}, f32[1,3,1792]{2,1,0:T(4,128)S(1)}, u32[]{:S(2)}, u32[]{:S(2)}) collective-permute-start(f32[1,3,1792]{2,1,0:T(4,128)} %slice.331), channel_id=1, source_target_pairs={{0,1},{1,2},{2,3},{3,4},{4,5},{5,6},{6,7},{8,9},{9,10},{10,11},{11... | collective-permute-start | bytes 64520 | tf_op jit(solution)/shard_map/ppermute | solution.py:13
  235.0 14.1 %collective-permute-start = (f32[1,24,64,128]{3,2,1,0:T(8,128)S(1)}, f32[1,24,64,128]{3,2,1,0:T(8,128)S(1)}, u32[]{:S(2)}, u32[]{:S(2)}) collective-permute-start(f32[1,24,64,128]{3,2,1,0:T(8,128)S(1)} %multiply_add_fusion.10), channel_id=1, source_target_pairs={{0,1},{1,2},{2,3},{3,4},{4,5},{5,6},{6,7},{8,9},{9,10},{10,11},{11... | collective-permute-start | bytes 2359304 | tf_op jit(solution)/shard_map/while/body/eval_jaxpr/ppermute | solution.py:13
  363.1 22.8 %collective-permute-start.5 = (f32[1,3,1792]{2,1,0:T(4,128)S(1)}, f32[1,3,1792]{2,1,0:T(4,128)S(1)}, u32[]{:S(2)}, u32[]{:S(2)}) collective-permute-start(f32[1,3,1792]{2,1,0:T(4,128)S(1)} %slice.345), channel_id=1, source_target_pairs={{0,1},{1,2},{2,3},{3,4},{4,5},{5,6},{6,7},{8,9},{9,10},{10,11},{11... | collective-permute-start | bytes 64520 | tf_op jit(solution)/shard_map/ppermute | solution.py:13
  549.4 458.5 %reduce-scatter.29.cloned.1.call-start = ((), (), s32[]{:S(2)}) async-start(), calls=%async_computation.15 | async-start | bytes 5898240 | tf_op jit(solution)/shard_map/reduce_scatter | solution.py:330
  570.9 437.0 %reduce-scatter.19.cloned.1.call-start = ((), (), s32[]{:S(2)}) async-start(), calls=%async_computation.10 | async-start | bytes 5898240 | tf_op jit(solution)/shard_map/reduce_scatter | solution.py:324
  590.5 14.3 %collective-permute-start.2 = (f32[1,24,64,128]{3,2,1,0:T(8,128)}, f32[1,24,64,128]{3,2,1,0:T(8,128)}, u32[]{:S(2)}, u32[]{:S(2)}) collective-permute-start(f32[1,24,64,128]{3,2,1,0:T(8,128)} %multiply_add_fusion.12), channel_id=1, source_target_pairs={{1,0},{2,1},{3,2},{4,3},{5,4},{6,5},{7,6},{9,8},{10,9},{11,10},{12... | collective-permute-start | bytes 2359304 | tf_op jit(solution)/shard_map/while/body/eval_jaxpr/ppermute | solution.py:13
  639.8 13.9 %collective-permute-start.2 = (f32[1,24,64,128]{3,2,1,0:T(8,128)}, f32[1,24,64,128]{3,2,1,0:T(8,128)}, u32[]{:S(2)}, u32[]{:S(2)}) collective-permute-start(f32[1,24,64,128]{3,2,1,0:T(8,128)} %multiply_add_fusion.12), channel_id=1, source_target_pairs={{1,0},{2,1},{3,2},{4,3},{5,4},{6,5},{7,6},{9,8},{10,9},{11,10},{12... | collective-permute-start | bytes 2359304 | tf_op jit(solution)/shard_map/while/body/eval_jaxpr/ppermute | solution.py:13
  739.8 23.4 %collective-permute-start.6 = (f32[1,3,1792]{2,1,0:T(4,128)}, f32[1,3,1792]{2,1,0:T(4,128)}, u32[]{:S(2)}, u32[]{:S(2)}) collective-permute-start(f32[1,3,1792]{2,1,0:T(4,128)} %slice.362), channel_id=1, source_target_pairs={{1,0},{2,1},{3,2},{4,3},{5,4},{6,5},{7,6},{9,8},{10,9},{11,10},{12... | collective-permute-start | bytes 64520 | tf_op jit(solution)/shard_map/ppermute | solution.py:13
  789.9 218.0 %reduce-scatter.27.cloned.1.call-start = ((), (), s32[]{:S(2)}) async-start(), calls=%async_computation.14 | async-start | bytes 5898240 | tf_op jit(solution)/shard_map/reduce_scatter | solution.py:330
  797.5 210.4 %reduce-scatter.25.cloned.1.call-start = ((), (), s32[]{:S(2)}) async-start(), calls=%async_computation.13 | async-start | bytes 6881280 | tf_op jit(solution)/shard_map/reduce_scatter | solution.py:325
  806.2 253.6 %reduce-scatter.23.cloned.1.call-start = ((), (), s32[]{:S(2)}) async-start(), calls=%async_computation.12 | async-start | bytes 6881280 | tf_op jit(solution)/shard_map/reduce_scatter | solution.py:325
  828.5 13.9 %collective-permute-start.3 = (f32[1,24,64,128]{3,2,1,0:T(8,128)}, f32[1,24,64,128]{3,2,1,0:T(8,128)S(1)}, u32[]{:S(2)}, u32[]{:S(2)}) collective-permute-start(f32[1,24,64,128]{3,2,1,0:T(8,128)} %multiply_add_fusion.13), channel_id=1, source_target_pairs={{1,0},{2,1},{3,2},{4,3},{5,4},{6,5},{7,6},{9,8},{10,9},{11,10},{12... | collective-permute-start | bytes 2359304 | tf_op jit(solution)/shard_map/while/body/eval_jaxpr/ppermute | solution.py:13
  994.6 150.8 %reduce-scatter.37.cloned.1.call-start = ((), (), s32[]{:S(2)}) async-start(), calls=%async_computation.25 | async-start | bytes 1146880
  996.6 149.8 %reduce-scatter.35.cloned.1.call-start = ((), (), s32[]{:S(2)}) async-start(), calls=%async_computation.24 | async-start | bytes 1146880
  998.1 150.0 %reduce-scatter.33.cloned.1.call-start = ((), (), s32[]{:S(2)}) async-start(), calls=%async_computation.23 | async-start | bytes 491520
  1000.4 174.8 %reduce-scatter.31.cloned.1.call-start = ((), (), s32[]{:S(2)}) async-start(), calls=%async_computation.22 | async-start | bytes 491520
  1007.8 331.4 %all-reduce.23.cloned.1.call-start = ((), (), s32[]{:S(2)}) async-start(), calls=%async_computation.26 | async-start | bytes 14942208 | tf_op jit(solution)/shard_map/psum | solution.py:332
  (193 other events, 2244.9 us)
Sparse Core Ops, SparseCore 0:
  11.0 76.4 all-gather.24
  89.3 60.5 all-gather.26
  151.8 57.1 all-gather.28
  210.7 65.1 all-gather.30
  277.6 57.0 all-gather.32
  336.4 57.0 all-gather.34
  549.6 67.0 reduce-scatter.20
  619.6 57.0 reduce-scatter.28
  790.0 66.9 reduce-scatter.18
  859.9 57.0 reduce-scatter.26
  920.1 63.6 reduce-scatter.24
  994.7 65.1 reduce-scatter.22
  1063.4 27.0 reduce-scatter.36
  1093.9 26.9 reduce-scatter.34
  1123.5 24.5 reduce-scatter.32
  1150.7 24.4 reduce-scatter.30
  1177.9 161.2 all-reduce.22
